TPU v7x, 32 devices: a whole 2x2x4 slice. The times are simulated.
32 devices in a mesh: ia: 2 (over y), ja: 4 (over z), ka: 4 (over x, core).
Axes of the slice: x: 2, y: 2, z: 4, core: 2. Of those that a mesh axis runs over, the one named last changes fastest.
Arguments:
- blocks: bfloat16 [256, 64, 4096], P(('ia', 'ja', 'ka')), may hold values from -12 to 12
- coords: int32 [256, 3], P(('ia', 'ja', 'ka')), may hold values from 0 to 63, as said below
- factor_one: float32 [2048, 512], P('ia'), may hold values from -1.2 to 1.2
- factor_two: float32 [4096, 512], P('ja'), may hold values from -1.2 to 1.2
- factor_three: float32 [4096, 512], P('ka'), may hold values from -1.2 to 1.2
Outputs:
- swept_one: float32 [2048, 512], P('ia')
- swept_two: float32 [4096, 512], P('ja')
- swept_three: float32 [4096, 512], P('ka')
Inputs may be any that keep to these rules, and one draw needn't show every extreme that they name: Row n of coords holds the three block coordinates of block n. The 8 rows of one device of ia+ja+ka (aligned blocks of 8 rows, devices in the order ia, ja, ka) have their second coordinate within that device's ja range (16 * ja to 16 * ja + 15) and their third within its ka range; at most 8 of them have a first coordinate within any one index of ia's range of 16; in every group of devices that share ja and ka, some index of ia receives exactly 8 from each device of the group. The same block may be listed more than once.
All inputs are finite; a program needn't handle non-finite values.
Results may differ from a plain program's by a relative error of at most 0.0028.
Values may be sent and summed in bfloat16 or wider, within the bound.
A program may use at most 64 MiB of HBM per device.

v0:
```python
import jax
import jax.numpy as jnp
from jax import lax
from jax.sharding import PartitionSpec as P

STEP_SIZE = 0.01
einsum_forms = (
    ("qk,rk->qrk", "pk,qrk->pqr", "pqr,qrk->pk"),
    ("pk,rk->prk", "qk,prk->pqr", "pqr,prk->qk"),
    ("pk,qk->pqk", "rk,pqk->pqr", "pqr,pqk->rk"),
)
other_modes = ((1, 2), (0, 2), (0, 1))


def block_gradient(cube, rows, mode):
    first, second = other_modes[mode]
    outer_form, model_form, grad_form = einsum_forms[mode]
    khatri = jnp.einsum(
        outer_form, rows[first].astype(jnp.float32), rows[second].astype(jnp.float32)
    ).astype(jnp.bfloat16)
    model = jnp.einsum(model_form, rows[mode], khatri, preferred_element_type=jnp.float32)
    misfit = (cube.astype(jnp.float32) - model).astype(jnp.bfloat16)
    return jnp.einsum(grad_form, misfit, khatri, preferred_element_type=jnp.float32)


def accumulate(blocks, coords, factors, starts, live, mode, height):
    edge = blocks.shape[1]
    width = factors[0].shape[1]

    def visit(index, total):

        def add(running):
            place = coords[index]
            rows = tuple(
                (
                    lax.dynamic_slice_in_dim(factors[f], place[f] * edge - starts[f], edge, 0)
                    for f in range(3)
                )
            )
            cube = blocks[index].reshape(edge, edge, edge)
            term = block_gradient(cube, rows, mode)
            offset = place[mode] * edge - starts[mode]
            current = lax.dynamic_slice_in_dim(running, offset, edge, 0)
            return lax.dynamic_update_slice_in_dim(running, current + term, offset, 0)

        return lax.cond(live[index], add, lambda running: running, total)

    empty = jnp.zeros((height, width), jnp.float32)
    return lax.fori_loop(0, blocks.shape[0], visit, empty)


def block_slots(coords, count, per_pair, held_rows):
    target = coords[:, 0] // held_rows
    same = target[:, None] == target[None, :]
    earlier = jnp.arange(count)[None, :] < jnp.arange(count)[:, None]
    before = jnp.sum((same & earlier).astype(jnp.int32), axis=1)
    return target * per_pair + before


def serve_rows(incoming, factor, edge, held_rows):
    width = factor.shape[1]
    within = incoming - lax.axis_index("ia") * held_rows
    safe_rows = jnp.clip(within, 0, held_rows - 1)
    picked = factor.astype(jnp.bfloat16).reshape(held_rows, edge, width)[safe_rows]
    return lax.all_to_all(picked, "ia", split_axis=0, concat_axis=0, tiled=True)


def per_device(blocks, coords, factor_one, factor_two, factor_three):
    edge = blocks.shape[1]
    count = blocks.shape[0]
    groups = lax.axis_size("ia")
    span_one = factor_one.shape[0]
    span_two = factor_two.shape[0]
    span_three = factor_three.shape[0]
    width = factor_one.shape[1]
    held_rows = span_one // edge
    per_pair = max(2, 2 * count // groups)
    start_two = lax.axis_index("ja") * span_two
    start_three = lax.axis_index("ka") * span_three
    slot = block_slots(coords, count, per_pair, held_rows)
    all_slots = groups * per_pair
    wanted = jnp.full((all_slots,), -1, jnp.int32).at[slot].set(coords[:, 0])
    incoming = lax.all_to_all(wanted, "ia", split_axis=0, concat_axis=0, tiled=True)
    fetched = serve_rows(incoming, factor_one, edge, held_rows).reshape(all_slots * edge, width)
    places = coords.at[:, 0].set(slot)
    live = jnp.ones((count,), jnp.bool_)
    slot_terms = accumulate(
        blocks,
        places,
        (fetched, factor_two.astype(jnp.bfloat16), factor_three.astype(jnp.bfloat16)),
        (0, start_two, start_three),
        live,
        0,
        all_slots * edge,
    )
    returned = lax.all_to_all(
        slot_terms.reshape(all_slots, edge, width), "ia", split_axis=0, concat_axis=0, tiled=True
    )
    within = incoming - lax.axis_index("ia") * held_rows
    selector = (within[None, :] == jnp.arange(held_rows)[:, None]).astype(jnp.float32)
    first_part = jnp.dot(
        selector,
        returned.reshape(all_slots, edge * width),
        precision=lax.Precision.HIGHEST,
        preferred_element_type=jnp.float32,
    ).reshape(span_one, width)
    first_part = lax.psum(first_part, ("ja", "ka"))
    factor_one = factor_one + STEP_SIZE * first_part
    first_rows = serve_rows(incoming, factor_one, edge, held_rows).reshape(
        groups * per_pair * edge, width
    )
    first_start = 0
    second_part = accumulate(
        blocks,
        places,
        (first_rows, factor_two.astype(jnp.bfloat16), factor_three.astype(jnp.bfloat16)),
        (first_start, start_two, start_three),
        live,
        1,
        span_two,
    )
    second_part = lax.psum(second_part, ("ia", "ka"))
    factor_two = factor_two + STEP_SIZE * second_part
    third_part = accumulate(
        blocks,
        places,
        (first_rows, factor_two.astype(jnp.bfloat16), factor_three.astype(jnp.bfloat16)),
        (first_start, start_two, start_three),
        live,
        2,
        span_three,
    )
    third_part = lax.psum(third_part, ("ia", "ja"))
    factor_three = factor_three + STEP_SIZE * third_part
    return (factor_one, factor_two, factor_three)


def solution(mesh):
    in_specs = (
        P(("ia", "ja", "ka"), None, None),
        P(("ia", "ja", "ka"), None),
        P("ia", None),
        P("ja", None),
        P("ka", None),
    )
    out_specs = (P("ia", None), P("ja", None), P("ka", None))
    return jax.shard_map(
        per_device, mesh=mesh, in_specs=in_specs, out_specs=out_specs, check_vma=False
    )
```

profile of v0, /device:TPU:0, one launch (start us, length us, event | category | flops | bytes accessed | tf_op | source)
XLA Modules:
  0.0 621.7 jit_solution(2798835930513432250)
XLA Ops:
  10.6 4.3 all-to-all-start
  27.9 8.9 %all-to-all-done.1 = bf16[16,64,512]{2,1,0:T(8,128)(2,1)S(1)} async-done(((bf16[16,64,512]{2,1,0:T(8,128)(2,1)}), bf16[16,64,512]{2,1,0:T(8,128)(2,1)S(1)}, u32[]{:S(2)}, u32[]{:S(2)}) %all-to-all-start.1) | async-done | bytes 1048608 | tf_op jit(solution)/shard_map/all_to_all | solution.py:65
  38.3 86.3 %while.40 = (s32[]{:T(128)}, f32[1024,512]{1,0:T(8,128)}, s32[8,3]{0,1:T(4,128)S(1)}, bf16[8,64,4096]{2,1,0:T(8,128)(2,1)}, bf16[1024,512]{1,0:T(8,128)(2,1)S(1)...) while((s32[]{:T(128)}, f32[1024,512]{1,0:T(8,128)}, ...), condition=%wide.region_4.5_spmd, body=%wide.region_3.4_spmd.sunk | while | flops 546144256 | bytes 15402399 | solution.py:49
  44.1 5.0 fusion.118
  54.8 5.0 fusion.118
  65.6 5.0 fusion.118
  76.4 5.0 fusion.118
  87.2 5.0 fusion.118
  98.0 5.0 fusion.118
  108.8 5.0 fusion.118
  119.6 5.0 fusion.118
  128.5 23.1 %all-to-all-done.2 = f32[16,64,512]{2,1,0:T(8,128)S(1)} async-done(((f32[16,64,512]{2,1,0:T(8,128)}), f32[16,64,512]{2,1,0:T(8,128)S(1)}, u32[]{:S(2)}, u32[]{:S(2)}) %all-to-all-start.2) | async-done | bytes 2097184 | tf_op jit(solution)/shard_map/all_to_all | solution.py:96
  155.5 98.7 %all-reduce.4.cloned.1.call-done = f32[1024,512]{1,0:T(8,128)} async-done(((f32[1024,512]{1,0:T(8,128)}), f32[1024,512]{1,0:T(8,128)}) %all-reduce.4.cloned.1.call-update) | async-done | bytes 2097168 | tf_op jit(solution)/shard_map/psum | solution.py:107
  259.3 4.4 all-to-all-start.3
  263.9 12.9 %all-to-all-done.3 = bf16[16,64,512]{2,1,0:T(8,128)(2,1)} async-done(((bf16[16,64,512]{2,1,0:T(8,128)(2,1)}), bf16[16,64,512]{2,1,0:T(8,128)(2,1)}, u32[]{:S(2)}, u32[]{:S(2)}) %all-to-all-start.3) | async-done | bytes 1048608 | tf_op jit(solution)/shard_map/all_to_all | solution.py:65
  278.4 92.2 %while.41 = (s32[]{:T(128)}, f32[1024,512]{1,0:T(8,128)}, s32[8,3]{0,1:T(4,128)S(1)}, s32[]{:T(128)}, bf16[8,64,4096]{2,1,0:T(8,128)(2,1)}, /*index=5*/s32[]{:T(...) while((s32[]{:T(128)}, f32[1024,512]{1,0:T(8,128)}, ...), condition=%wide.region_7.8_spmd, body=%wide.region_6.7_spmd.sunk | while | flops 546144256 | bytes 9110887 | solution.py:49
  285.6 4.4 fusion.123
  297.1 4.4 fusion.123
  308.6 4.4 fusion.123
  320.1 4.4 fusion.123
  331.6 4.4 fusion.123
  343.2 4.4 fusion.123
  354.7 4.4 fusion.123
  366.2 4.4 fusion.123
  370.6 59.9 %all-reduce.6.cloned.1.call-done = f32[1024,512]{1,0:T(8,128)} async-done(((f32[1024,512]{1,0:T(8,128)}), f32[1024,512]{1,0:T(8,128)}) %all-reduce.6.cloned.1.call-update) | async-done | bytes 2097168 | tf_op jit(solution)/shard_map/psum | solution.py:122
  435.6 74.6 %while.42 = (s32[]{:T(128)}, f32[1024,512]{1,0:T(8,128)}, s32[8,3]{0,1:T(4,128)S(1)}, s32[]{:T(128)}, bf16[8,64,4096]{2,1,0:T(8,128)(2,1)}, /*index=5*/s32[]{:T(...) while((s32[]{:T(128)}, f32[1024,512]{1,0:T(8,128)}, ...), condition=%wide.region_10.11_spmd, body=%wide.region_9.10_spmd.sunk | while | flops 546144256 | bytes 15402399 | solution.py:49
  469.1 3.8 fusion.128
  478.4 3.8 fusion.128
  487.7 3.8 fusion.128
  497.0 3.8 fusion.128
  506.4 3.8 fusion.128
  510.2 101.5 %all-reduce.8.cloned.1.call-done = f32[1024,512]{1,0:T(8,128)} async-done(((f32[1024,512]{1,0:T(8,128)}), f32[1024,512]{1,0:T(8,128)}) %all-reduce.8.cloned.1.call-update) | async-done | bytes 2097168 | tf_op jit(solution)/shard_map/psum | solution.py:133
  (240 shorter events, 152.5 us)
Async XLA Ops:
  10.6 8.0 %all-to-all-start = ((s32[2,8,1]{1,2,0:T(1,128)}), s32[2,8,1]{1,2,0:T(1,128)S(1)}, u32[]{:S(2)}, u32[]{:S(2)}) async-start(s32[2,8,1]{1,2,0:T(1,128)} %bitcast.29), calls=%async_computation | async-start | bytes 2048 | tf_op jit(solution)/shard_map/all_to_all | solution.py:83
  20.3 16.5 %all-to-all-start.1 = ((bf16[16,64,512]{2,1,0:T(8,128)(2,1)}), bf16[16,64,512]{2,1,0:T(8,128)(2,1)S(1)}, u32[]{:S(2)}, u32[]{:S(2)}) async-start(bf16[16,64,512]{2,1,0:T(8,128)(2,1)} %gather_fusion), calls=%async_computation.1 | async-start | bytes 2097152 | tf_op jit(solution)/shard_map/all_to_all | solution.py:65
  44.1 5.1 copy-start.7
  49.1 3.8 copy-start.6
  54.8 5.1 copy-start.7
  59.9 3.8 copy-start.6
  65.6 5.1 copy-start.7
  70.7 3.8 copy-start.6
  76.4 5.1 copy-start.7
  81.5 3.8 copy-start.6
  87.2 5.1 copy-start.7
  92.3 3.8 copy-start.6
  98.0 5.1 copy-start.7
  103.0 3.8 copy-start.6
  108.8 5.1 copy-start.7
  119.6 5.1 copy-start.7
  124.6 27.0 %all-to-all-start.2 = ((f32[16,64,512]{2,1,0:T(8,128)}), f32[16,64,512]{2,1,0:T(8,128)S(1)}, u32[]{:S(2)}, u32[]{:S(2)}) async-start(f32[16,64,512]{2,1,0:T(8,128)} %bitcast.175), calls=%async_computation.2 | async-start | bytes 4194304 | tf_op jit(solution)/shard_map/all_to_all | solution.py:96
  128.4 125.9 %all-reduce.4.cloned.1.call-start = ((), (), s32[]{:S(2)}) async-start(), calls=%async_computation.4 | async-start | bytes 4194304 | tf_op jit(solution)/shard_map/psum | solution.py:107
  155.5 98.8 %copy-start = (f32[1024,512]{1,0:T(8,128)S(1)}, f32[1024,512]{1,0:T(8,128)}, u32[]{:S(2)}) copy-start(f32[1024,512]{1,0:T(8,128)} %param.15) | copy-start | bytes 6291460
  259.3 17.6 %all-to-all-start.3 = ((bf16[16,64,512]{2,1,0:T(8,128)(2,1)}), bf16[16,64,512]{2,1,0:T(8,128)(2,1)}, u32[]{:S(2)}, u32[]{:S(2)}) async-start(bf16[16,64,512]{2,1,0:T(8,128)(2,1)} %gather_fusion.1), calls=%async_computation.3 | async-start | bytes 2097152 | tf_op jit(solution)/shard_map/all_to_all | solution.py:65
  263.7 166.9 %all-reduce.6.cloned.1.call-start = ((), (), s32[]{:S(2)}) async-start(), calls=%async_computation.5 | async-start | bytes 4194304 | tf_op jit(solution)/shard_map/psum | solution.py:122
  370.6 60.0 %copy-start.2 = (f32[1024,512]{1,0:T(8,128)S(1)}, f32[1024,512]{1,0:T(8,128)}, u32[]{:S(2)}) copy-start(f32[1024,512]{1,0:T(8,128)} %param.16) | copy-start | bytes 6291460
  370.6 241.1 %all-reduce.8.cloned.1.call-start = ((), (), s32[]{:S(2)}) async-start(), calls=%async_computation.6 | async-start | bytes 4194304 | tf_op jit(solution)/shard_map/psum | solution.py:133
  441.1 3.8 copy-start.5
  450.4 3.8 copy-start.5
  459.7 3.8 copy-start.5
  469.0 3.8 copy-start.5
  478.4 3.8 copy-start.5
  487.7 3.8 copy-start.5
  497.0 3.8 copy-start.5
  506.4 3.8 copy-start.5
  510.2 101.5 %copy-start.3 = (f32[1024,512]{1,0:T(8,128)S(1)}, f32[1024,512]{1,0:T(8,128)}, u32[]{:S(2)}) copy-start(f32[1024,512]{1,0:T(8,128)} %param.17) | copy-start | bytes 6291460
  (11 other events, 38.6 us)
Sparse Core Ops, SparseCore 0:
  155.6 98.5 all-reduce.3
  370.7 59.7 all-reduce.5
  510.3 101.3 all-reduce.7
where the time goes:
time: 626 us; the launch traced here: 622 us
  waiting for transfers between devices  307 us (49%)
  matrix products  107 us (17%)
  other arithmetic  65.5 us (10%)
  local copies, waits for them, and re-layouts  64.8 us (10%)
  loops' own time  47.1 us (8%)
  starting transfers between devices  16.3 us (3%)
  between operations  13.8 us (2%)
    dot_general x24, matrix products, block_gradient(): jnp.einsum(grad_form, misfit, khatri, preferred_element_type=jnp.float32)  106 us
    psum x1, waiting for transfers between devices, per_device(): third_part = lax.psum(third_part, ('ia', 'ja'))  102 us
    psum x1, waiting for transfers between devices, per_device(): first_part = lax.psum(first_part, ('ja', 'ka'))  98.7 us
    psum x1, waiting for transfers between devices, per_device(): second_part = lax.psum(second_part, ('ia', 'ka'))  59.9 us
    another operation x3, loops' own time, accumulate(): return lax.fori_loop(0, blocks.shape[0], visit, empty)  47.1 us
    convert_element_type x32, local copies, waits for them, and re-layouts, block_gradient(): misfit = (cube.astype(jnp.float32) - model).astype(jnp.bfloat16)  34.5 us
    convert_element_type x24, other arithmetic, block_gradient(): misfit = (cube.astype(jnp.float32) - model).astype(jnp.bfloat16)  26.8 us
    all_to_all x1, waiting for transfers between devices, per_device(): lax.all_to_all(slot_terms.reshape(all_slots, edge, width), 'ia', split_ax...  23.1 us
  transfers between devices with their start and end apart: 7, of which 7 were waited for; matrix products, arithmetic and copies ran while one was open for 1% of the time, Pallas kernels for 0%

commit v1 on v0

--- a/solution.py
+++ b/solution.py
@@ -104,7 +104,7 @@
         precision=lax.Precision.HIGHEST,
         preferred_element_type=jnp.float32,
     ).reshape(span_one, width)
-    first_part = lax.psum(first_part, ("ja", "ka"))
+    first_part = lax.psum(lax.psum(first_part, "ka"), "ja")
     factor_one = factor_one + STEP_SIZE * first_part
     first_rows = serve_rows(incoming, factor_one, edge, held_rows).reshape(
         groups * per_pair * edge, width

time: 626 us -> 669 us (1.069)
  waiting for transfers between devices: 307 us -> 350 us
    psum x1 -> x2, waiting for transfers between devices: 98.7 us -> 140 us  [per_device(): first_part = lax.psum(lax.psum(first_part, 'ka'), 'ja')]
  transfers between devices with their start and end apart: 7 -> 8, of which waited for: 7 -> 8; matrix products, arithmetic and copies ran while one was open for 1% -> 1% of each run, Pallas kernels for 0% -> 0%
where the time goes in v1:
time: 669 us; the launch traced here: 665 us
  waiting for transfers between devices  350 us (52%)
  matrix products  107 us (16%)
  other arithmetic  65.5 us (10%)
  local copies, waits for them, and re-layouts  64.8 us (10%)
  loops' own time  47.9 us (7%)
  starting transfers between devices  16.4 us (2%)
  between operations  13.8 us (2%)
    psum x2, waiting for transfers between devices, per_device(): first_part = lax.psum(lax.psum(first_part, 'ka'), 'ja')  140 us
    dot_general x24, matrix products, block_gradient(): jnp.einsum(grad_form, misfit, khatri, preferred_element_type=jnp.float32)  106 us
    psum x1, waiting for transfers between devices, per_device(): third_part = lax.psum(third_part, ('ia', 'ja'))  102 us
    psum x1, waiting for transfers between devices, per_device(): second_part = lax.psum(second_part, ('ia', 'ka'))  60.4 us
    another operation x3, loops' own time, accumulate(): return lax.fori_loop(0, blocks.shape[0], visit, empty)  47.9 us
    convert_element_type x32, local copies, waits for them, and re-layouts, block_gradient(): misfit = (cube.astype(jnp.float32) - model).astype(jnp.bfloat16)  34.5 us
    convert_element_type x24, other arithmetic, block_gradient(): misfit = (cube.astype(jnp.float32) - model).astype(jnp.bfloat16)  26.8 us
    all_to_all x1, waiting for transfers between devices, per_device(): lax.all_to_all(slot_terms.reshape(all_slots, edge, width), 'ia', split_ax...  23.1 us
  transfers between devices with their start and end apart: 8, of which 8 were waited for; matrix products, arithmetic and copies ran while one was open for 1% of the time, Pallas kernels for 0%

profile of v1, /device:TPU:0, one launch (start us, length us, event | category | flops | bytes accessed | tf_op | source)
XLA Modules:
  0.0 665.1 jit_solution(5888735727909697752)
XLA Ops:
  10.6 4.3 all-to-all-start
  27.9 8.8 %all-to-all-done.1 = bf16[16,64,512]{2,1,0:T(8,128)(2,1)S(1)} async-done(((bf16[16,64,512]{2,1,0:T(8,128)(2,1)}), bf16[16,64,512]{2,1,0:T(8,128)(2,1)S(1)}, u32[]{:S(2)}, u32[]{:S(2)}) %all-to-all-start.1) | async-done | bytes 1048608 | tf_op jit(solution)/shard_map/all_to_all | solution.py:65
  38.3 84.7 %while.40 = (s32[]{:T(128)}, f32[1024,512]{1,0:T(8,128)}, s32[8,3]{0,1:T(4,128)S(1)}, bf16[8,64,4096]{2,1,0:T(8,128)(2,1)}, bf16[1024,512]{1,0:T(8,128)(2,1)S(1)...) while((s32[]{:T(128)}, f32[1024,512]{1,0:T(8,128)}, ...), condition=%wide.region_4.5_spmd, body=%wide.region_3.4_spmd.sunk | while | flops 546144256 | bytes 15402399 | solution.py:49
  43.9 5.0 fusion.118
  54.5 5.0 fusion.118
  65.1 5.0 fusion.118
  75.6 5.0 fusion.118
  86.2 5.0 fusion.118
  96.8 5.0 fusion.118
  107.4 5.0 fusion.118
  118.0 5.0 fusion.118
  126.9 23.1 %all-to-all-done.2 = f32[16,64,512]{2,1,0:T(8,128)S(1)} async-done(((f32[16,64,512]{2,1,0:T(8,128)}), f32[16,64,512]{2,1,0:T(8,128)S(1)}, u32[]{:S(2)}, u32[]{:S(2)}) %all-to-all-start.2) | async-done | bytes 2097184 | tf_op jit(solution)/shard_map/all_to_all | solution.py:96
  154.0 51.8 %all-reduce.5.cloned.1.call-done = f32[1024,512]{1,0:T(8,128)} async-done(((f32[1024,512]{1,0:T(8,128)}), f32[1024,512]{1,0:T(8,128)}) %all-reduce.5.cloned.1.call-update) | async-done | bytes 2097168 | tf_op jit(solution)/shard_map/psum | solution.py:107
  205.8 88.6 %all-reduce.7.cloned.1.call-done = f32[1024,512]{1,0:T(8,128)} async-done(((f32[1024,512]{1,0:T(8,128)}), f32[1024,512]{1,0:T(8,128)}) %all-reduce.7.cloned.1.call-update) | async-done | bytes 2097168 | tf_op jit(solution)/shard_map/psum | solution.py:107
  299.4 4.4 all-to-all-start.3
  304.1 13.4 %all-to-all-done.3 = bf16[16,64,512]{2,1,0:T(8,128)(2,1)} async-done(((bf16[16,64,512]{2,1,0:T(8,128)(2,1)}), bf16[16,64,512]{2,1,0:T(8,128)(2,1)}, u32[]{:S(2)}, u32[]{:S(2)}) %all-to-all-start.3) | async-done | bytes 1048608 | tf_op jit(solution)/shard_map/all_to_all | solution.py:65
  319.1 94.3 %while.41 = (s32[]{:T(128)}, f32[1024,512]{1,0:T(8,128)}, s32[8,3]{0,1:T(4,128)S(1)}, s32[]{:T(128)}, bf16[8,64,4096]{2,1,0:T(8,128)(2,1)}, /*index=5*/s32[]{:T(...) while((s32[]{:T(128)}, f32[1024,512]{1,0:T(8,128)}, ...), condition=%wide.region_8.9_spmd, body=%wide.region_7.8_spmd.sunk | while | flops 546144256 | bytes 9110887 | solution.py:49
  326.5 4.4 fusion.123
  338.3 4.4 fusion.123
  350.0 4.4 fusion.123
  361.8 4.4 fusion.123
  373.6 4.4 fusion.123
  385.4 4.4 fusion.123
  397.2 4.4 fusion.123
  409.0 4.4 fusion.123
  413.4 60.4 %all-reduce.9.cloned.1.call-done = f32[1024,512]{1,0:T(8,128)} async-done(((f32[1024,512]{1,0:T(8,128)}), f32[1024,512]{1,0:T(8,128)}) %all-reduce.9.cloned.1.call-update) | async-done | bytes 2097168 | tf_op jit(solution)/shard_map/psum | solution.py:122
  478.8 74.8 %while.42 = (s32[]{:T(128)}, f32[1024,512]{1,0:T(8,128)}, s32[8,3]{0,1:T(4,128)S(1)}, s32[]{:T(128)}, bf16[8,64,4096]{2,1,0:T(8,128)(2,1)}, /*index=5*/s32[]{:T(...) while((s32[]{:T(128)}, f32[1024,512]{1,0:T(8,128)}, ...), condition=%wide.region_11.12_spmd, body=%wide.region_10.11_spmd.sunk | while | flops 546144256 | bytes 15402399 | solution.py:49
  503.1 3.8 fusion.128
  521.8 3.8 fusion.128
  540.5 3.8 fusion.128
  549.8 3.8 fusion.128
  553.7 101.5 %all-reduce.11.cloned.1.call-done = f32[1024,512]{1,0:T(8,128)} async-done(((f32[1024,512]{1,0:T(8,128)}), f32[1024,512]{1,0:T(8,128)}) %all-reduce.11.cloned.1.call-update) | async-done | bytes 2097168 | tf_op jit(solution)/shard_map/psum | solution.py:133
  (243 shorter events, 156.5 us)
Async XLA Ops:
  10.6 8.0 %all-to-all-start = ((s32[2,8,1]{1,2,0:T(1,128)}), s32[2,8,1]{1,2,0:T(1,128)S(1)}, u32[]{:S(2)}, u32[]{:S(2)}) async-start(s32[2,8,1]{1,2,0:T(1,128)} %bitcast.29), calls=%async_computation | async-start | bytes 2048 | tf_op jit(solution)/shard_map/all_to_all | solution.py:83
  20.3 16.5 %all-to-all-start.1 = ((bf16[16,64,512]{2,1,0:T(8,128)(2,1)}), bf16[16,64,512]{2,1,0:T(8,128)(2,1)S(1)}, u32[]{:S(2)}, u32[]{:S(2)}) async-start(bf16[16,64,512]{2,1,0:T(8,128)(2,1)} %gather_fusion), calls=%async_computation.1 | async-start | bytes 2097152 | tf_op jit(solution)/shard_map/all_to_all | solution.py:65
  43.9 5.1 copy-start.7
  48.9 3.6 copy-start.6
  54.4 5.1 copy-start.7
  59.5 3.6 copy-start.6
  65.0 5.1 copy-start.7
  70.1 3.6 copy-start.6
  75.6 5.1 copy-start.7
  80.7 3.6 copy-start.6
  86.2 5.1 copy-start.7
  91.3 3.6 copy-start.6
  96.8 5.1 copy-start.7
  107.4 5.1 copy-start.7
  118.0 5.1 copy-start.7
  123.0 27.0 %all-to-all-start.2 = ((f32[16,64,512]{2,1,0:T(8,128)}), f32[16,64,512]{2,1,0:T(8,128)S(1)}, u32[]{:S(2)}, u32[]{:S(2)}) async-start(f32[16,64,512]{2,1,0:T(8,128)} %bitcast.175), calls=%async_computation.2 | async-start | bytes 4194304 | tf_op jit(solution)/shard_map/all_to_all | solution.py:96
  126.8 79.0 %all-reduce.5.cloned.1.call-start = ((), (), s32[]{:S(2)}) async-start(), calls=%async_computation.4 | async-start | bytes 4194304 | tf_op jit(solution)/shard_map/psum | solution.py:107
  153.9 140.5 %copy-start = (f32[1024,512]{1,0:T(8,128)S(1)}, f32[1024,512]{1,0:T(8,128)}, u32[]{:S(2)}) copy-start(f32[1024,512]{1,0:T(8,128)} %param.15) | copy-start | bytes 6291460
  154.0 140.5 %all-reduce.7.cloned.1.call-start = ((), (), s32[]{:S(2)}) async-start(), calls=%async_computation.5 | async-start | bytes 4194304 | tf_op jit(solution)/shard_map/psum | solution.py:107
  299.4 18.1 %all-to-all-start.3 = ((bf16[16,64,512]{2,1,0:T(8,128)(2,1)}), bf16[16,64,512]{2,1,0:T(8,128)(2,1)}, u32[]{:S(2)}, u32[]{:S(2)}) async-start(bf16[16,64,512]{2,1,0:T(8,128)(2,1)} %gather_fusion.1), calls=%async_computation.3 | async-start | bytes 2097152 | tf_op jit(solution)/shard_map/all_to_all | solution.py:65
  303.9 170.0 %all-reduce.9.cloned.1.call-start = ((), (), s32[]{:S(2)}) async-start(), calls=%async_computation.6 | async-start | bytes 4194304 | tf_op jit(solution)/shard_map/psum | solution.py:122
  413.4 60.5 %copy-start.2 = (f32[1024,512]{1,0:T(8,128)S(1)}, f32[1024,512]{1,0:T(8,128)}, u32[]{:S(2)}) copy-start(f32[1024,512]{1,0:T(8,128)} %param.16) | copy-start | bytes 6291460
  413.4 241.8 %all-reduce.11.cloned.1.call-start = ((), (), s32[]{:S(2)}) async-start(), calls=%async_computation.7 | async-start | bytes 4194304 | tf_op jit(solution)/shard_map/psum | solution.py:133
  484.3 3.8 copy-start.5
  493.7 3.8 copy-start.5
  503.1 3.8 copy-start.5
  512.4 3.8 copy-start.5
  521.8 3.8 copy-start.5
  531.1 3.8 copy-start.5
  540.5 3.8 copy-start.5
  549.8 3.8 copy-start.5
  553.7 101.5 %copy-start.3 = (f32[1024,512]{1,0:T(8,128)S(1)}, f32[1024,512]{1,0:T(8,128)}, u32[]{:S(2)}) copy-start(f32[1024,512]{1,0:T(8,128)} %param.17) | copy-start | bytes 6291460
  (12 other events, 42.1 us)
Sparse Core Ops, SparseCore 0:
  154.1 51.6 all-reduce.4
  208.2 86.1 all-reduce.6
  413.5 60.2 all-reduce.8
  553.8 101.3 all-reduce.10
